TPU v7x, 32 devices: a whole 2x2x4 slice. The times are simulated.
32 devices in a mesh: row: 8 (over y, x, core), col: 4 (over z).
Axes of the slice: x: 2, y: 2, z: 4, core: 2. Of those that a mesh axis runs over, the one named last changes fastest.
Arguments:
- columns: float32 [16384, 1024], P('row', 'col'), as said below
Outputs:
- factored: float32 [16384, 1024], P('row', 'col')
- projected: float32 [256, 1024], P(None, 'col')
Inputs may be any that keep to these rules, and one draw needn't show every extreme that they name: `columns`: the panel has full column rank and a condition number of at most about 40.
All inputs are finite; a program needn't handle non-finite values.
Results may differ from a plain program's by a relative error of at most 0.0003.
Values sent between devices are 32-bit elements; how exact they have to be, the bound alone decides.
No kernel may reach another device: no remote copies, remote signals or barrier semaphores. Data moves between devices by JAX's collectives and lax.ppermute only.
A program may use at most 64 MiB of HBM per device.

v0:
```python
import jax
import jax.numpy as jnp
from jax import lax
from jax.sharding import PartitionSpec as P


def spread(value, axis, source):
    kept = jnp.where(lax.axis_index(axis) == source, value, 0).astype(value.dtype)
    return lax.psum(kept, axis)


def cross_product(left, right):
    return lax.dot_general(
        left,
        right,
        (((0,), (0,)), ((), ())),
        precision=lax.Precision.HIGHEST,
        preferred_element_type=jnp.float32,
    )


def invert_lower(gram_sum):
    lower = jnp.linalg.cholesky(gram_sum)
    ident = jnp.eye(gram_sum.shape[0], dtype=jnp.float32)
    return jax.scipy.linalg.solve_triangular(lower, ident, lower=True)


def times_inverse(block, inverse):
    return jnp.dot(
        block, inverse.T, precision=lax.Precision.HIGHEST, preferred_element_type=jnp.float32
    )


def per_device(columns):
    at_root = lax.axis_index("col") == 0
    panel_rows = spread(columns, "col", 0)
    gram_sum, raw_proj = lax.psum(
        (cross_product(panel_rows, panel_rows), cross_product(panel_rows, columns)), "row"
    )
    inverse_low = invert_lower(gram_sum)
    sent_basis = times_inverse(panel_rows, inverse_low)
    projected = jnp.dot(
        inverse_low, raw_proj, precision=lax.Precision.HIGHEST, preferred_element_type=jnp.float32
    )
    remainder = columns - jnp.dot(
        sent_basis, projected, precision=lax.Precision.HIGHEST, preferred_element_type=jnp.float32
    )
    factored = jnp.where(at_root, sent_basis, remainder)
    return (factored, projected)


def solution(mesh):
    return jax.shard_map(
        per_device,
        mesh=mesh,
        in_specs=(P("row", "col"),),
        out_specs=(P("row", "col"), P(None, "col")),
        check_vma=False,
    )
```

profile of v0, /device:TPU:0, one launch (start us, length us, event | category | flops | bytes accessed | tf_op | source)
XLA Modules:
  0.0 239.8 jit_solution(14196477842423527275)
XLA Ops:
  7.2 0.0 all-reduce.5.cloned.1.call-start
  7.2 3.1 %broadcast_select_fusion = f32[2048,256]{1,0:T(8,128)} fusion(f32[2048,256]{1,0:T(8,128)} %param.1, pred[]{:T(512)S(6)} %eq.9), kind=kLoop, calls=%fused_computation.6 | loop fusion | flops 524288 | bytes 4194305 | tf_op jit(solution)/shard_map/jit(_where)/select_n | solution.py:8
  10.3 0.0 all-reduce.5.cloned.1.call-update
  10.3 0.0 all-reduce.7.cloned.1.call-start
  10.3 89.4 %all-reduce.5.cloned.1.call-done = f32[2048,256]{1,0:T(8,128)} async-done(((f32[2048,256]{1,0:T(8,128)}), f32[2048,256]{1,0:T(8,128)}) %all-reduce.5.cloned.1.call-update) | async-done | bytes 2097168 | tf_op jit(solution)/shard_map/psum | solution.py:9
  99.8 0.0 copy-start
  99.8 6.5 %fusion.15 = f32[256,256]{1,0:T(8,128)} fusion(f32[2048,256]{1,0:T(8,128)} %all-reduce.5.cloned.1.call-done, f32[2048,256]{1,0:T(8,128)} %param.1), kind=kOutput, calls=%fused_computation.38 | convolution fusion | flops 1610612736 | bytes 4456448 | tf_op jit(solution)/shard_map/dot_general | solution.py:13
  106.3 0.0 copy-done
  106.3 4.2 %fusion.14 = f32[256,256]{0,1:T(8,128)} fusion(f32[2048,256]{1,0:T(8,128)S(1)} %copy-done), kind=kOutput, calls=%fused_computation.37 | convolution fusion | flops 1610612736 | bytes 2359296 | tf_op jit(solution)/shard_map/dot_general | solution.py:13
  110.5 0.0 all-reduce.7.cloned.1.call-update
  110.6 54.0 %all-reduce.7.cloned.1.call-done = (f32[256,256]{0,1:T(8,128)}, f32[256,256]{1,0:T(8,128)}) async-done(((f32[256,256]{0,1:T(8,128)}, f32[256,256]{1,0:T(8,128)}), (f32[256,256]{0,1:T(8,128)}, f32[256,256]{1,0:T(8,128)})) %all-reduce.7.cloned.1.call-update) | async-done | bytes 524304 | tf_op jit(solution)/shard_map/psum | solution.py:37
  164.6 1.1 copy.4
  165.7 0.0 copy-start.3
  165.7 1.0 fusion.1
  166.7 11.7 %cholesky.50 = f32[128,128]{1,0:T(8,128)S(1)} custom-call(f32[128,128]{1,0:T(8,128)S(1)} %cholesky.118), custom_call_target="Cholesky" | custom-call | tf_op jit(solution)/shard_map/jit(cholesky)/cholesky | solution.py:23
  178.5 10.0 %custom-call.15 = f32[1,128,128]{1,2,0:T(8,128)S(1)} custom-call(f32[1,128,128]{2,1,0:T(8,128)S(1)} %get-tuple-element.25), custom_call_target="InvertDiagBlocksLowerTriangular" | custom-call | tf_op jit(solution)/shard_map/jit(cholesky)/cholesky | solution.py:23
  188.4 0.2 constant_dynamic-update-slice_fusion.1
  188.6 0.3 convolution_subtract_fusion.2
  188.9 11.7 %cholesky.105 = f32[128,128]{1,0:T(8,128)S(1)} custom-call(f32[128,128]{1,0:T(8,128)S(1)} %convolution_subtract_fusion.2), custom_call_target="Cholesky" | custom-call | tf_op jit(solution)/shard_map/jit(cholesky)/cholesky | solution.py:23
  200.7 0.6 compare_reduce_fusion
  202.7 0.1 triangular_solve.63
  202.7 4.0 %while.1 = (s32[]{:T(128)}, f32[256,256]{1,0:T(8,128)S(1)}, s32[2,2]{1,0:T(2,128)S(1)}, f32[2,128,128]{2,1,0:T(8,128)S(1)}, s32[]{:T(128)}) while((s32[]{:T(128)}, f32[256,256]{1,0:T(8,128)S(1)}, s32[2,2]{1,0:T(2,128)S(1)}, f32[2,128,128]{2,1,0:T(8,128)S(1)}, s32[]{:T(128)}) %tuple.27), condition=%wide.while_cond, body=%wide.while_body.sunk | while | flops 2 | bytes 131189 | solution.py:25
  202.7 0.6 fusion.29
  203.3 1.4 bitcast_dynamic-update-slice_fusion.2
  204.7 0.6 fusion.29
  205.3 1.4 bitcast_dynamic-update-slice_fusion.2
  206.7 19.7 %custom-call.16 = f32[2,128,128]{1,2,0:T(8,128)S(1)} custom-call(f32[2,128,128]{2,1,0:T(8,128)S(1)} %get-tuple-element.9), custom_call_target="InvertDiagBlocksLowerTriangular" | custom-call | tf_op jit(solution)/shard_map/jit(_solve_triangular)/triangular_solve | solution.py:25
  226.4 0.3 fusion.4
  226.7 0.3 convolution_subtract_fusion.1
  226.9 0.3 fusion.7
  227.3 0.0 copy-done.3
  227.3 0.4 fusion.2
  227.7 0.0 copy-start.2
  227.7 0.0 copy-start.1
  227.7 1.9 fusion.3
  229.6 0.0 copy-done.2
  229.6 0.0 copy-done.1
  229.7 3.3 %fusion = f32[2048,256]{1,0:T(8,128)} fusion(f32[2048,256]{1,0:T(8,128)S(1)} %fusion.3, f32[2048,256]{1,0:T(8,128)S(1)} %copy-done.1, f32[256,256]{1,0:T(8,128)S(1)} %fusion.2, pred[]{:T(512)S(6)} %eq.9), kind=kOutput, calls=%fused_computation.3 | convolution fusion | flops 1611661312 | bytes 6553601 | tf_op jit(solution)/shard_map/dot_general | solution.py:45
  (10 shorter events, 0.2 us)
Async XLA Ops:
  7.2 92.6 %all-reduce.5.cloned.1.call-start = ((), (), s32[]{:S(2)}) async-start(), calls=%async_computation | async-start | bytes 4194304 | tf_op jit(solution)/shard_map/psum | solution.py:9
  10.3 154.3 %all-reduce.7.cloned.1.call-start = ((), (), s32[]{:S(2)}) async-start(), calls=%async_computation.1 | async-start | bytes 1048576 | tf_op jit(solution)/shard_map/psum | solution.py:37
  99.8 6.5 %copy-start = (f32[2048,256]{1,0:T(8,128)S(1)}, f32[2048,256]{1,0:T(8,128)}, u32[]{:S(2)}) copy-start(f32[2048,256]{1,0:T(8,128)} %all-reduce.5.cloned.1.call-done) | copy-start | bytes 6291460
  165.7 61.6 %copy-start.3 = (f32[256,256]{1,0:T(8,128)S(1)}, f32[256,256]{1,0:T(8,128)}, u32[]{:S(2)}) copy-start(f32[256,256]{1,0:T(8,128)} %get-tuple-element.19) | copy-start | bytes 786436
  227.7 2.0 copy-start.2
  227.7 2.0 copy-start.1
Sparse Core Ops, SparseCore 0:
  10.9 88.8 all-reduce.4
  110.6 53.8 all-reduce.6
where the time goes:
time: 240 us
  waiting for transfers between devices  143 us (60%)
  other arithmetic  57.9 us (24%)
  matrix products  17.6 us (7%)
  between operations  15.5 us (6%)
  local copies, waits for them, and re-layouts  5.15 us (2%)
    psum x1, waiting for transfers between devices, spread(): return lax.psum(kept, axis)  89.4 us
    psum x1, waiting for transfers between devices, per_device(): lax.psum((cross_product(panel_rows, panel_rows), cross_product(panel_rows...  54 us
    another operation x6, other arithmetic, invert_lower(): lower = jnp.linalg.cholesky(gram_sum)  34.1 us
    another operation x3, other arithmetic, invert_lower(): return jax.scipy.linalg.solve_triangular(lower, ident, lower=True)  19.7 us
    dot_general x2, matrix products, cross_product(): lax.dot_general(left, right, (((0,), (0,)), ((), ())), precision=lax.Prec...  10.7 us
  transfers between devices with their start and end apart: 2, of which 2 were waited for; matrix products, arithmetic and copies ran while one was open for 0% of the time, Pallas kernels for 0%

commit v1 on v0

--- a/solution.py
+++ b/solution.py
@@ -6,7 +6,7 @@
 
 def spread(value, axis, source):
     kept = jnp.where(lax.axis_index(axis) == source, value, 0).astype(value.dtype)
-    return lax.psum(kept, axis)
+    return jnp.sum(lax.all_gather(kept, axis), axis=0)
 
 
 def cross_product(left, right):

time: 240 us -> 304 us (1.27)
  waiting for transfers between devices: 143 us -> 205 us
  other arithmetic: 57.9 us -> 62 us
    all_gather x0 -> x1, waiting for transfers between devices: none -> 152 us  [spread(): return jnp.sum(lax.all_gather(kept, axis), axis=0)]
    psum x1 -> x0, waiting for transfers between devices: 89.4 us -> none  [spread(): return lax.psum(kept, axis)]
    reduce_sum x0 -> x1, other arithmetic: none -> 4.21 us  [spread(): return jnp.sum(lax.all_gather(kept, axis), axis=0)]
where the time goes in v1:
time: 304 us
  waiting for transfers between devices  205 us (67%)
  other arithmetic  62 us (20%)
  between operations  15.5 us (5%)
  matrix products  15.2 us (5%)
  local copies, waits for them, and re-layouts  5.15 us (2%)
    all_gather x1, waiting for transfers between devices, spread(): return jnp.sum(lax.all_gather(kept, axis), axis=0)  152 us
    psum x1, waiting for transfers between devices, per_device(): lax.psum((cross_product(panel_rows, panel_rows), cross_product(panel_rows...  53.1 us
    another operation x6, other arithmetic, invert_lower(): lower = jnp.linalg.cholesky(gram_sum)  34.1 us
    another operation x3, other arithmetic, invert_lower(): return jax.scipy.linalg.solve_triangular(lower, ident, lower=True)  19.7 us
    dot_general x2, matrix products, cross_product(): lax.dot_general(left, right, (((0,), (0,)), ((), ())), precision=lax.Prec...  8.35 us
  transfers between devices with their start and end apart: 2, of which 2 were waited for; matrix products, arithmetic and copies ran while one was open for 0% of the time, Pallas kernels for 0%

profile of v1, /device:TPU:0, one launch (start us, length us, event | category | flops | bytes accessed | tf_op | source)
XLA Modules:
  0.0 303.6 jit_solution(7921908181354726277)
XLA Ops:
  7.2 0.0 all-gather.3.cloned.1.call-start
  7.2 3.1 %broadcast_select_fusion = f32[2048,256]{1,0:T(8,128)} fusion(f32[2048,256]{1,0:T(8,128)} %param.1, pred[]{:T(512)S(6)} %eq.9), kind=kLoop, calls=%fused_computation.6 | loop fusion | flops 524288 | bytes 4194305 | tf_op jit(solution)/shard_map/jit(_where)/select_n | solution.py:8
  10.3 0.0 all-gather.3.cloned.1.call-update
  10.3 0.0 all-reduce.4.cloned.1.call-start
  10.3 152.1 %all-gather.3.cloned.1.call-done = f32[8192,256]{1,0:T(8,128)} async-done(((f32[2048,256]{1,0:T(8,128)}), f32[8192,256]{1,0:T(8,128)}) %all-gather.3.cloned.1.call-update) | async-done | bytes 8388624 | tf_op jit(solution)/shard_map/all_gather | solution.py:9
  162.5 4.2 %reduce_sum.9 = f32[2048,256]{1,0:T(8,128)S(1)} reduce(f32[4,2048,256]{2,1,0:T(8,128)} %bitcast.40, f32[]{:T(128)} %constant.82.clone.1), dimensions={0}, to_apply=%region_0.1 | reduce | flops 1572864 | bytes 10485764 | tf_op jit(solution)/shard_map/reduce_sum | solution.py:9
  166.7 0.0 copy-start
  166.7 4.2 %fusion.14 = f32[256,256]{0,1:T(8,128)} fusion(f32[2048,256]{1,0:T(8,128)S(1)} %reduce_sum.9), kind=kOutput, calls=%fused_computation.37 | convolution fusion | flops 1610612736 | bytes 2359296 | tf_op jit(solution)/shard_map/dot_general | solution.py:13
  170.9 0.0 copy-done
  170.9 4.2 %fusion.15 = f32[256,256]{1,0:T(8,128)} fusion(f32[2048,256]{1,0:T(8,128)S(1)} %reduce_sum.9, f32[2048,256]{1,0:T(8,128)S(1)} %copy-done), kind=kOutput, calls=%fused_computation.38 | convolution fusion | flops 1610612736 | bytes 4456448 | tf_op jit(solution)/shard_map/dot_general | solution.py:13
  175.1 0.0 all-reduce.4.cloned.1.call-update
  175.1 53.1 %all-reduce.4.cloned.1.call-done = (f32[256,256]{0,1:T(8,128)}, f32[256,256]{1,0:T(8,128)}) async-done(((f32[256,256]{0,1:T(8,128)}, f32[256,256]{1,0:T(8,128)}), (f32[256,256]{0,1:T(8,128)}, f32[256,256]{1,0:T(8,128)})) %all-reduce.4.cloned.1.call-update) | async-done | bytes 524304 | tf_op jit(solution)/shard_map/psum | solution.py:37
  228.3 1.1 copy.4
  229.4 1.0 fusion.1
  230.4 11.7 %cholesky.50 = f32[128,128]{1,0:T(8,128)S(1)} custom-call(f32[128,128]{1,0:T(8,128)S(1)} %cholesky.118), custom_call_target="Cholesky" | custom-call | tf_op jit(solution)/shard_map/jit(cholesky)/cholesky | solution.py:23
  242.1 9.9 %custom-call.15 = f32[1,128,128]{1,2,0:T(8,128)S(1)} custom-call(f32[1,128,128]{2,1,0:T(8,128)S(1)} %get-tuple-element.25), custom_call_target="InvertDiagBlocksLowerTriangular" | custom-call | tf_op jit(solution)/shard_map/jit(cholesky)/cholesky | solution.py:23
  252.1 0.2 constant_dynamic-update-slice_fusion.1
  252.3 0.3 convolution_subtract_fusion.2
  252.5 11.7 %cholesky.105 = f32[128,128]{1,0:T(8,128)S(1)} custom-call(f32[128,128]{1,0:T(8,128)S(1)} %convolution_subtract_fusion.2), custom_call_target="Cholesky" | custom-call | tf_op jit(solution)/shard_map/jit(cholesky)/cholesky | solution.py:23
  264.3 0.6 compare_reduce_fusion
  266.3 0.1 triangular_solve.63
  266.3 4.2 %while.1 = (s32[]{:T(128)}, f32[256,256]{1,0:T(8,128)S(1)}, s32[2,2]{1,0:T(2,128)S(1)}, f32[2,128,128]{2,1,0:T(8,128)S(1)}, s32[]{:T(128)}) while((s32[]{:T(128)}, f32[256,256]{1,0:T(8,128)S(1)}, s32[2,2]{1,0:T(2,128)S(1)}, f32[2,128,128]{2,1,0:T(8,128)S(1)}, s32[]{:T(128)}) %tuple.27), condition=%wide.while_cond, body=%wide.while_body.sunk | while | flops 2 | bytes 131181 | solution.py:25
  266.5 0.6 fusion.29
  267.1 1.4 bitcast_dynamic-update-slice_fusion.2
  268.5 0.6 fusion.29
  269.1 1.4 bitcast_dynamic-update-slice_fusion.2
  270.5 19.7 %custom-call.16 = f32[2,128,128]{1,2,0:T(8,128)S(1)} custom-call(f32[2,128,128]{2,1,0:T(8,128)S(1)} %get-tuple-element.9), custom_call_target="InvertDiagBlocksLowerTriangular" | custom-call | tf_op jit(solution)/shard_map/jit(_solve_triangular)/triangular_solve | solution.py:25
  290.2 0.3 fusion.4
  290.5 0.3 convolution_subtract_fusion.1
  290.7 0.3 fusion.7
  291.1 0.0 copy-start.3
  291.1 0.0 copy-start.1
  291.1 1.9 fusion.3
  293.0 0.0 copy-done.3
  293.0 0.4 fusion.2
  293.4 0.0 copy-done.1
  293.4 0.0 copy-start.2
  293.4 3.3 %fusion = f32[2048,256]{1,0:T(8,128)} fusion(f32[2048,256]{1,0:T(8,128)S(1)} %fusion.3, f32[2048,256]{1,0:T(8,128)S(1)} %copy-done.1, f32[256,256]{1,0:T(8,128)S(1)} %fusion.2, pred[]{:T(512)S(6)} %eq.9), kind=kOutput, calls=%fused_computation.3 | convolution fusion | flops 1611661312 | bytes 6553601 | tf_op jit(solution)/shard_map/dot_general | solution.py:45
  296.7 0.0 copy-done.2
  (10 shorter events, 0.2 us)
Async XLA Ops:
  7.2 155.3 %all-gather.3.cloned.1.call-start = ((), (), s32[]{:S(2)}) async-start(), calls=%async_computation | async-start | bytes 10485760 | tf_op jit(solution)/shard_map/all_gather | solution.py:9
  10.3 218.0 %all-reduce.4.cloned.1.call-start = ((), (), s32[]{:S(2)}) async-start(), calls=%async_computation.1 | async-start | bytes 1048576 | tf_op jit(solution)/shard_map/psum | solution.py:37
  166.7 4.2 %copy-start = (f32[2048,256]{1,0:T(8,128)S(1)}, f32[2048,256]{1,0:T(8,128)}, u32[]{:S(2)}) copy-start(f32[2048,256]{1,0:T(8,128)} %param.1) | copy-start | bytes 6291460
  291.1 2.0 copy-start.3
  291.1 2.4 copy-start.1
  293.4 3.3 %copy-start.2 = (f32[256,256]{1,0:T(8,128)}, f32[256,256]{1,0:T(8,128)S(1)}, u32[]{:S(2)}) copy-start(f32[256,256]{1,0:T(8,128)S(1)} %fusion.2) | copy-start | bytes 786436
Sparse Core Ops, SparseCore 0:
  10.4 152.0 all-gather.2
  175.2 53.0 all-reduce.3
